TPU v7x, 256 devices: a whole 4x4x8 slice. The times are simulated.
256 devices in a mesh: row: 16 (over y_lo, z), col: 16 (over y_hi, x, core).
Axes of the slice: x: 4, y: 4 (y_hi: 2, y_lo: 2; y = y_hi * 2 + y_lo), z: 8, core: 2. Of those that a mesh axis runs over, the one named last changes fastest.
Arguments:
- env: float32 [1024, 32768], P('row', 'col'), may hold values from -0.03125 to 0.03125
- wave: float32 [32768, 2048], P('row', 'col'), may hold values from -6 to 6
- mpo: float32 [16, 16], replicated, may hold values from -1.5 to 1.5
Outputs:
- applied: float32 [1024, 2048], P('row', 'col')
All inputs are finite; a program needn't handle non-finite values.
Results may differ from a plain program's by a relative error of at most 0.00007.
Values sent between devices are 32-bit elements; how exact they have to be, the bound alone decides.
A program may use at most 128 MiB of HBM per device.

v0:
```python
import jax
import jax.numpy as jnp
from jax import lax
from jax.sharding import PartitionSpec as P


def shards(env, wave, mpo):
    n = lax.axis_size("row")
    spins = mpo.shape[0]
    swap = [(a * n + b, b * n + a) for a in range(n) for b in range(n)]
    moved = lax.ppermute(env, ("row", "col"), swap)
    env_k = lax.all_gather(moved, "col", axis=0, tiled=True)
    part = jnp.dot(env_k, wave, precision=lax.Precision.HIGHEST, preferred_element_type=jnp.float32)
    block = lax.psum_scatter(part, "row", scatter_dimension=0, tiled=True)
    rows = block.shape[0]
    mixed = jnp.einsum(
        "irs,st->tir", block.reshape(rows, -1, spins), mpo, precision=lax.Precision.HIGHEST
    )
    spun = lax.all_to_all(mixed, "col", split_axis=0, concat_axis=2, tiled=True)
    return spun.reshape(rows, -1)


def solution(mesh):
    in_specs = (P("row", "col"), P("row", "col"), P())
    out_specs = P("row", "col")
    return jax.shard_map(shards, mesh=mesh, in_specs=in_specs, out_specs=out_specs, check_vma=False)
```

profile of v0, /device:TPU:1, one launch (start us, length us, event | category | flops | bytes accessed | tf_op | source)
XLA Modules:
  0.0 232.7 jit_solution(1275761468202975840)
XLA Ops:
  6.5 0.0 copy-start
  6.5 0.0 copy-start.2
  6.5 0.0 all-gather.2.cloned.1.call-start
  6.5 5.1 %collective-permute-start = (f32[64,2048]{1,0:T(8,128)}, f32[64,2048]{1,0:T(8,128)S(1)}, u32[]{:S(2)}, u32[]{:S(2)}) collective-permute-start(f32[64,2048]{1,0:T(8,128)} %param.3), channel_id=1, source_target_pairs={{0,0},{1,16},{2,32},{3,48},{4,64},{5,80},{6,96},{7,112},{8,128},{9... | collective-permute-start | bytes 1572872 | tf_op jit(solution)/shard_map/ppermute | solution.py:11
  11.6 9.1 %collective-permute-done = f32[64,2048]{1,0:T(8,128)S(1)} collective-permute-done((f32[64,2048]{1,0:T(8,128)}, f32[64,2048]{1,0:T(8,128)S(1)}, u32[]{:S(2)}, u32[]{:S(2)}) %collective-permute-start) | collective-permute-done | bytes 524320 | tf_op jit(solution)/shard_map/ppermute | solution.py:11
  20.7 0.0 copy-start.1
  20.7 0.8 copy-done.1
  21.6 0.0 all-gather.2.cloned.1.call-update
  21.6 0.0 reduce-scatter.2.cloned.1.call-start
  21.6 108.9 %all-gather.2.cloned.1.call-done = f32[1024,2048]{1,0:T(8,128)} async-done(((f32[64,2048]{1,0:T(8,128)}), f32[1024,2048]{1,0:T(8,128)}) %all-gather.2.cloned.1.call-update) | async-done | bytes 8388624 | tf_op jit(solution)/shard_map/all_gather | solution.py:12
  130.5 0.0 copy-done
  130.5 9.7 %fusion.1 = f32[1024,128]{1,0:T(8,128)} fusion(f32[1024,2048]{1,0:T(8,128)} %all-gather.2.cloned.1.call-done, f32[2048,128]{1,0:T(8,128)S(1)} %copy-done), kind=kOutput, calls=%fused_computation.4 | convolution fusion | flops 3221225472 | bytes 9961472 | tf_op jit(solution)/shard_map/dot_general | solution.py:13
  140.3 0.0 reduce-scatter.2.cloned.1.call-update
  140.3 56.2 %reduce-scatter.2.cloned.1.call-done = f32[64,128]{1,0:T(8,128)} async-done(((f32[1024,128]{1,0:T(8,128)}), f32[64,128]{1,0:T(8,128)}) %reduce-scatter.2.cloned.1.call-update) | async-done | bytes 32784 | tf_op jit(solution)/shard_map/reduce_scatter | solution.py:14
  196.5 0.8 copy.10
  197.4 0.0 copy-done.2
  197.4 0.3 convolution_bitcast_fusion
  197.7 0.1 reshape.10
  197.8 26.0 %all_to_all.15 = f32[16,1,512]{2,1,0:T(1,128)S(1)} all-to-all(f32[16,1,512]{2,1,0:T(1,128)S(1)} %reshape.10), channel_id=1, replica_groups=mesh['row'=16,'col'=16] {'col'}, dimensions={0} | all-to-all | bytes 65536 | tf_op jit(solution)/shard_map/all_to_all | solution.py:19
  223.8 0.5 broadcast
  224.3 0.7 reduce
  225.1 0.1 reshape.11
  225.2 0.7 copy.13
  (2 shorter events, 0.0 us)
Async XLA Ops:
  6.5 124.0 %copy-start = (f32[2048,128]{1,0:T(8,128)S(1)}, f32[2048,128]{1,0:T(8,128)}, u32[]{:S(2)}) copy-start(f32[2048,128]{1,0:T(8,128)} %param.4) | copy-start | bytes 3145732
  6.5 190.9 %copy-start.2 = (f32[16,16]{1,0:T(8,128)S(1)}, f32[16,16]{1,0:T(8,128)}, u32[]{:S(2)}) copy-start(f32[16,16]{1,0:T(8,128)} %param.5) | copy-start | bytes 3076
  6.5 124.0 %all-gather.2.cloned.1.call-start = ((), (), s32[]{:S(2)}) async-start(), calls=%async_computation.2 | async-start | bytes 8912896 | tf_op jit(solution)/shard_map/all_gather | solution.py:12
  6.5 14.2 %collective-permute-start = (f32[64,2048]{1,0:T(8,128)}, f32[64,2048]{1,0:T(8,128)S(1)}, u32[]{:S(2)}, u32[]{:S(2)}) collective-permute-start(f32[64,2048]{1,0:T(8,128)} %param.3), channel_id=1, source_target_pairs={{0,0},{1,16},{2,32},{3,48},{4,64},{5,80},{6,96},{7,112},{8,128},{9... | collective-permute-start | bytes 1572872 | tf_op jit(solution)/shard_map/ppermute | solution.py:11
  20.7 0.8 copy-start.1
  21.6 175.0 %reduce-scatter.2.cloned.1.call-start = ((), (), s32[]{:S(2)}) async-start(), calls=%async_computation.3 | async-start | bytes 557056 | tf_op jit(solution)/shard_map/reduce_scatter | solution.py:14
Sparse Core Ops, SparseCore 0:
  21.7 108.7 all-gather.1
  140.4 56.0 reduce-scatter.1
where the time goes:
time: 233 us
  waiting for transfers between devices  174 us (75%)
  blocking collectives  26 us (11%)
  between operations  13.5 us (6%)
  matrix products  10 us (4%)
  starting transfers between devices  5.1 us (2%)
  local copies, waits for them, and re-layouts  3.12 us (1%)
    all_gather x1, waiting for transfers between devices, shards(): env_k = lax.all_gather(moved, 'col', axis=0, tiled=True)  109 us
    reduce_scatter x1, waiting for transfers between devices, shards(): block = lax.psum_scatter(part, 'row', scatter_dimension=0, tiled=True)  56.2 us
    all_to_all x1, blocking collectives, shards(): spun = lax.all_to_all(mixed, 'col', split_axis=0, concat_axis=2, tiled=True)  26 us
    dot_general x1, matrix products, shards(): jnp.dot(env_k, wave, precision=lax.Precision.HIGHEST, preferred_element_t...  9.75 us
    ppermute x1, waiting for transfers between devices, shards(): moved = lax.ppermute(env, ('row', 'col'), swap)  9.1 us
    ppermute x1, starting transfers between devices, shards(): moved = lax.ppermute(env, ('row', 'col'), swap)  5.05 us
  transfers between devices with their start and end apart: 3, of which 3 were waited for; matrix products, arithmetic and copies ran while one was open for 0% of the time, Pallas kernels for 0%

commit v1 on v0

--- a/solution.py
+++ b/solution.py
@@ -9,7 +9,9 @@
     spins = mpo.shape[0]
     swap = [(a * n + b, b * n + a) for a in range(n) for b in range(n)]
     moved = lax.ppermute(env, ("row", "col"), swap)
-    env_k = lax.all_gather(moved, "col", axis=0, tiled=True)
+    env_k = jnp.concatenate(
+        lax.all_to_all(jnp.stack([moved] * lax.axis_size("col")), "col", 0, 0), axis=0
+    )
     part = jnp.dot(env_k, wave, precision=lax.Precision.HIGHEST, preferred_element_type=jnp.float32)
     block = lax.psum_scatter(part, "row", scatter_dimension=0, tiled=True)
     rows = block.shape[0]

time: 233 us -> 254 us (1.090)
  blocking collectives: 26 us -> 158 us
  waiting for transfers between devices: 174 us -> 65.6 us
    all_to_all x0 -> x1, blocking collectives: none -> 132 us  [shards(): lax.all_to_all(jnp.stack([moved] * lax.axis_size('col')), 'col', 0, 0)]
    all_gather x1 -> x0, waiting for transfers between devices: 109 us -> none  [shards(): env_k = lax.all_gather(moved, 'col', axis=0, tiled=True)]
  transfers between devices with their start and end apart: 3 -> 2, of which waited for: 3 -> 2; matrix products, arithmetic and copies ran while one was open for 0% -> 0% of each run, Pallas kernels for 0% -> 0%
where the time goes in v1:
time: 254 us; the launch traced here: 253 us
  blocking collectives  158 us (62%)
  waiting for transfers between devices  65.6 us (26%)
  between operations  13.5 us (5%)
  matrix products  7.73 us (3%)
  starting transfers between devices  5.06 us (2%)
  local copies, waits for them, and re-layouts  3.3 us (1%)
    all_to_all x1, blocking collectives, shards(): lax.all_to_all(jnp.stack([moved] * lax.axis_size('col')), 'col', 0, 0)  132 us
    reduce_scatter x1, waiting for transfers between devices, shards(): block = lax.psum_scatter(part, 'row', scatter_dimension=0, tiled=True)  56.4 us
    all_to_all x1, blocking collectives, shards(): spun = lax.all_to_all(mixed, 'col', split_axis=0, concat_axis=2, tiled=True)  25.8 us
    ppermute x1, waiting for transfers between devices, shards(): moved = lax.ppermute(env, ('row', 'col'), swap)  9.1 us
    dot_general x1, matrix products, shards(): jnp.dot(env_k, wave, precision=lax.Precision.HIGHEST, preferred_element_t...  7.48 us
  transfers between devices with their start and end apart: 2, of which 2 were waited for; matrix products, arithmetic and copies ran while one was open for 0% of the time, Pallas kernels for 0%

profile of v1, /device:TPU:1, one launch (start us, length us, event | category | flops | bytes accessed | tf_op | source)
XLA Modules:
  0.0 253.3 jit_solution(3675710535790347957)
XLA Ops:
  6.5 0.0 copy-start
  6.5 0.0 reduce-scatter.2.cloned.1.call-start
  6.5 5.1 %collective-permute-start = (f32[64,2048]{1,0:T(8,128)}, f32[64,2048]{1,0:T(8,128)S(1)}, u32[]{:S(2)}, u32[]{:S(2)}) collective-permute-start(f32[64,2048]{1,0:T(8,128)} %param.3), channel_id=1, source_target_pairs={{0,0},{1,16},{2,32},{3,48},{4,64},{5,80},{6,96},{7,112},{8,128},{9... | collective-permute-start | bytes 1572872 | tf_op jit(solution)/shard_map/ppermute | solution.py:11
  11.6 9.1 %collective-permute-done = f32[64,2048]{1,0:T(8,128)S(1)} collective-permute-done((f32[64,2048]{1,0:T(8,128)}, f32[64,2048]{1,0:T(8,128)S(1)}, u32[]{:S(2)}, u32[]{:S(2)}) %collective-permute-start) | collective-permute-done | bytes 524320 | tf_op jit(solution)/shard_map/ppermute | solution.py:11
  20.7 1.0 stack.2
  21.7 131.7 %all_to_all.20 = f32[16,64,2048]{2,1,0:T(8,128)S(1)} all-to-all(f32[16,64,2048]{2,1,0:T(8,128)S(1)} %stack.2), channel_id=1, replica_groups=mesh['row'=16,'col'=16] {'col'}, dimensions={0} | all-to-all | bytes 16777216 | tf_op jit(solution)/shard_map/all_to_all | solution.py:13
  153.4 0.0 copy-start.1
  153.4 0.0 copy-done
  153.4 7.5 %fusion.1 = f32[1024,128]{1,0:T(8,128)} fusion(f32[1024,2048]{1,0:T(8,128)S(1)} %bitcast.21, f32[2048,128]{1,0:T(8,128)S(1)} %copy-done), kind=kOutput, calls=%fused_computation.4 | convolution fusion | flops 3221225472 | bytes 9961472 | tf_op jit(solution)/shard_map/dot_general | solution.py:15
  160.9 0.0 reduce-scatter.2.cloned.1.call-update
  160.9 56.4 %reduce-scatter.2.cloned.1.call-done = f32[64,128]{1,0:T(8,128)} async-done(((f32[1024,128]{1,0:T(8,128)}), f32[64,128]{1,0:T(8,128)}) %reduce-scatter.2.cloned.1.call-update) | async-done | bytes 32784 | tf_op jit(solution)/shard_map/reduce_scatter | solution.py:16
  217.4 0.8 copy.10
  218.2 0.0 copy-done.1
  218.2 0.3 convolution_bitcast_fusion
  218.5 0.1 reshape.16
  218.6 25.8 %all_to_all.21 = f32[16,1,512]{2,1,0:T(1,128)S(1)} all-to-all(f32[16,1,512]{2,1,0:T(1,128)S(1)} %reshape.16), channel_id=1, replica_groups=mesh['row'=16,'col'=16] {'col'}, dimensions={0} | all-to-all | bytes 65536 | tf_op jit(solution)/shard_map/all_to_all | solution.py:21
  244.5 0.5 broadcast.2
  245.0 0.7 reduce
  245.7 0.1 reshape.17
  245.8 0.7 copy.13
  (2 shorter events, 0.0 us)
Async XLA Ops:
  6.5 146.9 %copy-start = (f32[2048,128]{1,0:T(8,128)S(1)}, f32[2048,128]{1,0:T(8,128)}, u32[]{:S(2)}) copy-start(f32[2048,128]{1,0:T(8,128)} %param.4) | copy-start | bytes 3145732
  6.5 210.8 %reduce-scatter.2.cloned.1.call-start = ((), (), s32[]{:S(2)}) async-start(), calls=%async_computation.3 | async-start | bytes 557056 | tf_op jit(solution)/shard_map/reduce_scatter | solution.py:16
  6.5 14.2 %collective-permute-start = (f32[64,2048]{1,0:T(8,128)}, f32[64,2048]{1,0:T(8,128)S(1)}, u32[]{:S(2)}, u32[]{:S(2)}) collective-permute-start(f32[64,2048]{1,0:T(8,128)} %param.3), channel_id=1, source_target_pairs={{0,0},{1,16},{2,32},{3,48},{4,64},{5,80},{6,96},{7,112},{8,128},{9... | collective-permute-start | bytes 1572872 | tf_op jit(solution)/shard_map/ppermute | solution.py:11
  153.4 64.8 %copy-start.1 = (f32[16,16]{1,0:T(8,128)S(1)}, f32[16,16]{1,0:T(8,128)}, u32[]{:S(2)}) copy-start(f32[16,16]{1,0:T(8,128)} %param.5) | copy-start | bytes 3076
Sparse Core Ops, SparseCore 0:
  161.0 56.2 reduce-scatter.1
